TPU v7x, 256 devices: a whole 4x4x8 slice. The times are simulated.
256 devices in a mesh: row: 8 (over z_hi, y), col: 32 (over z_lo, x, core).
Axes of the slice: x: 4, y: 4, z: 8 (z_hi: 2, z_lo: 4; z = z_hi * 4 + z_lo), core: 2. Of those that a mesh axis runs over, the one named last changes fastest.
Arguments:
- queries: bfloat16 [32768, 256], P(('row', 'col')), may hold values from -6 to 6
- keys: bfloat16 [32768, 256], P('col', 'row'), may hold values from -6 to 6
- values: bfloat16 [32768, 256], P('col', 'row'), may hold values from -0.59765625 to 0.59765625
- outputs: bfloat16 [32768, 256], P(('row', 'col')), may hold values from -0.59765625 to 0.59765625
- d_out: bfloat16 [32768, 256], P(('row', 'col')), may hold values from -6 to 6
- lse: float32 [2, 32768], P(None, ('row', 'col')), may hold values from 4 to 6
Outputs:
- d_queries: bfloat16 [32768, 256], P(('row', 'col'))
- d_keys: bfloat16 [32768, 256], P('col', 'row')
- d_values: bfloat16 [32768, 256], P('col', 'row')
All inputs are finite; a program needn't handle non-finite values.
Results may differ from a plain program's by a relative error of at most 0.0049.
Values may be sent and summed in bfloat16 or wider, within the bound.
No kernel may reach another device: no remote copies, remote signals or barrier semaphores. Data moves between devices by JAX's collectives and lax.ppermute only.
A program may use at most 64 MiB of HBM per device.

v0:
```python
import jax
import jax.numpy as jnp
from jax import lax
from jax.sharding import PartitionSpec as P


def block_size(row_total):
    block_rows = row_total
    while block_rows > 512 and block_rows % 2 == 0:
        block_rows = block_rows // 2
    return block_rows


def head_slice(matrix, head_index, head_dim):
    return matrix[:, head_index * head_dim : (head_index + 1) * head_dim]


def contract_rows(left, right):
    return lax.dot_general(
        left, right, (((0,), (0,)), ((), ())), preferred_element_type=jnp.float32
    )


def score_terms(query_head, grad_head, lse_row, delta_row, key_head, value_head, scaling):
    scores = jnp.dot(query_head, key_head.T, preferred_element_type=jnp.float32)
    probs = jnp.exp(scores * scaling - lse_row[:, None])
    probs_low = probs.astype(jnp.bfloat16)
    grad_probs = jnp.dot(grad_head, value_head.T, preferred_element_type=jnp.float32)
    grad_scores = (probs * (grad_probs - delta_row[:, None])).astype(jnp.bfloat16)
    return (probs_low, grad_scores)


def block_grads(query_rows, grad_rows, lse_rows, delta_rows, key_all, value_all, head_dim):
    head_total = lse_rows.shape[0]
    scaling = head_dim ** (-0.5)
    key_terms = []
    value_terms = []
    query_terms = []
    for head_index in range(head_total):
        query_head = head_slice(query_rows, head_index, head_dim)
        grad_head = head_slice(grad_rows, head_index, head_dim)
        key_head = head_slice(key_all, head_index, head_dim)
        value_head = head_slice(value_all, head_index, head_dim)
        probs_low, grad_scores = score_terms(
            query_head,
            grad_head,
            lse_rows[head_index],
            delta_rows[head_index],
            key_head,
            value_head,
            scaling,
        )
        value_terms.append(contract_rows(probs_low, grad_head))
        key_terms.append(contract_rows(grad_scores, query_head))
        query_terms.append(jnp.dot(grad_scores, key_head, preferred_element_type=jnp.float32))
    key_term = jnp.concatenate(key_terms, axis=1)
    value_term = jnp.concatenate(value_terms, axis=1)
    query_term = jnp.concatenate(query_terms, axis=1)
    return (key_term, value_term, query_term)


def split_blocks(query_all, grad_all, lse_all, delta_all):
    row_total, features = query_all.shape
    block_rows = block_size(row_total)
    steps_total = row_total // block_rows
    head_total = lse_all.shape[0]
    query_blocks = query_all.reshape(steps_total, block_rows, features)
    grad_blocks = grad_all.reshape(steps_total, block_rows, features)
    lse_blocks = lse_all.reshape(head_total, steps_total, block_rows).transpose(1, 0, 2)
    delta_blocks = delta_all.reshape(head_total, steps_total, block_rows).transpose(1, 0, 2)
    return (query_blocks, grad_blocks, lse_blocks, delta_blocks)


def query_pass(query_all, grad_all, lse_all, delta_all, key_all, value_all, head_dim):
    row_total, features = query_all.shape
    block_inputs = split_blocks(query_all, grad_all, lse_all, delta_all)
    empty_sums = jnp.zeros((key_all.shape[0], features), jnp.float32)

    def advance(running, inputs):
        key_sum, value_sum = running
        query_rows, grad_rows, lse_rows, delta_rows = inputs
        key_term, value_term, query_term = block_grads(
            query_rows, grad_rows, lse_rows, delta_rows, key_all, value_all, head_dim
        )
        return ((key_sum + key_term, value_sum + value_term), query_term)

    (key_sum, value_sum), query_terms = lax.scan(advance, (empty_sums, empty_sums), block_inputs)
    query_terms = query_terms.reshape(row_total, features)
    return (key_sum, value_sum, query_terms)


def head_delta(d_out, outputs, head_total, head_dim):
    product = d_out.astype(jnp.float32) * outputs.astype(jnp.float32)
    return jnp.sum(product.reshape(product.shape[0], head_total, head_dim), axis=2).T


def per_device(queries, keys, values, outputs, d_out, lse):
    head_total = lse.shape[0]
    head_dim = queries.shape[1] // head_total
    scaling = head_dim ** (-0.5)
    delta = head_delta(d_out, outputs, head_total, head_dim)
    key_all, value_all = (
        lax.all_gather(keys, "row", axis=1, tiled=True),
        lax.all_gather(values, "row", axis=1, tiled=True),
    )
    query_all, grad_all = (
        lax.all_gather(queries, "col", axis=0, tiled=True),
        lax.all_gather(d_out, "col", axis=0, tiled=True),
    )
    lse_all, delta_all = (
        lax.all_gather(lse, "col", axis=1, tiled=True),
        lax.all_gather(delta, "col", axis=1, tiled=True),
    )
    key_sum, value_sum, query_terms = query_pass(
        query_all, grad_all, lse_all, delta_all, key_all, value_all, head_dim
    )
    query_grad = lax.psum_scatter(query_terms, "col", scatter_dimension=0, tiled=True)
    key_grad, value_grad = (
        lax.psum_scatter(key_sum, "row", scatter_dimension=1, tiled=True),
        lax.psum_scatter(value_sum, "row", scatter_dimension=1, tiled=True),
    )
    d_queries = (query_grad * scaling).astype(jnp.bfloat16)
    d_keys = (key_grad * scaling).astype(jnp.bfloat16)
    d_values = value_grad.astype(jnp.bfloat16)
    return (d_queries, d_keys, d_values)


def solution(mesh):
    placed = (
        P(("row", "col"), None),
        P("col", "row"),
        P("col", "row"),
        P(("row", "col"), None),
        P(("row", "col"), None),
        P(None, ("row", "col")),
    )
    return jax.shard_map(
        per_device,
        mesh=mesh,
        in_specs=placed,
        out_specs=(P(("row", "col"), None), P("col", "row"), P("col", "row")),
        check_vma=False,
    )
```

profile of v0, /device:TPU:8, one launch (start us, length us, event | category | flops | bytes accessed | tf_op | source)
XLA Modules:
  0.0 613.3 jit_solution(17690217975706771563)
XLA Ops:
  9.7 47.4 %all_gather.19 = bf16[1024,256]{0,1:T(8,128)(2,1)S(1)} all-gather(bf16[1024,32]{0,1:T(8,128)(2,1)} %param.9), channel_id=1, replica_groups=mesh['row'=8,'col'=32] {'row'}, dimensions={1}, use_global_device_ids=true | all-gather | bytes 589824 | tf_op jit(solution)/shard_map/all_gather | solution.py:103
  57.4 45.8 %all_gather.22 = bf16[1024,256]{0,1:T(8,128)(2,1)S(1)} all-gather(bf16[1024,32]{0,1:T(8,128)(2,1)S(1)} %copy-done.1), channel_id=1, replica_groups=mesh['row'=8,'col'=32] {'row'}, dimensions={1}, use_global_device_ids=true | all-gather | bytes 589824 | tf_op jit(solution)/shard_map/all_gather | solution.py:104
  103.6 50.5 %all_gather.23 = f32[2,4096]{0,1:T(8,128)} all-gather(f32[2,128]{0,1:T(8,128)S(1)} %bitcast.55), channel_id=1, replica_groups=mesh['row'=8,'col'=32] {'col'}, dimensions={1}, use_global_device_ids=true | all-gather | bytes 33792 | tf_op jit(solution)/shard_map/all_gather | solution.py:112
  154.1 2.2 copy.19
  156.3 37.9 %all_gather.20 = f32[2,4096]{1,0:T(2,128)S(1)} all-gather(f32[2,128]{1,0:T(2,128)S(1)} %copy-done.2), channel_id=1, replica_groups=mesh['row'=8,'col'=32] {'col'}, dimensions={1}, use_global_device_ids=true | all-gather | bytes 33792 | tf_op jit(solution)/shard_map/all_gather | solution.py:111
  194.2 87.0 %while.15 = (s32[]{:T(128)}, f32[1024,256]{0,1:T(8,128)}, f32[1024,256]{0,1:T(8,128)S(1)}, f32[8,512,256]{2,1,0:T(8,128)}, bf16[8,512,256]{2,1,0:T(8,128)(2,1)},...) while((s32[]{:T(128)}, f32[1024,256]{0,1:T(8,128)}, ...), condition=%wide.region_2.3_spmd.clone, body=%wide.region_1.2_spmd.clone.sunk | while | flops 1352269824 | bytes 34631860 | solution.py:87
  194.3 1.0 dynamic-slice_bitcast_fusion.5
  195.2 1.0 dynamic-slice_bitcast_fusion.4
  201.2 1.8 maximum_add_fusion.3
  204.1 1.0 dynamic-slice_bitcast_fusion.5
  205.0 1.0 dynamic-slice_bitcast_fusion.4
  211.0 3.0 maximum_add_fusion.3
  215.1 1.0 dynamic-slice_bitcast_fusion.5
  216.0 1.0 dynamic-slice_bitcast_fusion.4
  222.0 3.0 maximum_add_fusion.3
  227.1 1.0 dynamic-slice_bitcast_fusion.4
  233.1 3.0 maximum_add_fusion.3
  237.2 1.0 dynamic-slice_bitcast_fusion.5
  238.1 1.0 dynamic-slice_bitcast_fusion.4
  244.1 3.0 maximum_add_fusion.3
  249.2 1.0 dynamic-slice_bitcast_fusion.4
  255.1 3.0 maximum_add_fusion.3
  259.2 1.0 dynamic-slice_bitcast_fusion.5
  266.2 3.0 maximum_add_fusion.3
  271.2 1.0 dynamic-slice_bitcast_fusion.4
  277.2 3.0 maximum_add_fusion.3
  283.4 85.4 %reduce-scatter.8.cloned.1.call-done = f32[1024,32]{0,1:T(8,128)} async-done(((f32[1024,256]{0,1:T(8,128)}), f32[1024,32]{0,1:T(8,128)}) %reduce-scatter.8.cloned.1.call-update) | async-done | bytes 131088 | tf_op jit(solution)/shard_map/reduce_scatter | solution.py:120
  368.8 1.5 convert_element_type.31
  370.3 85.5 %reduce-scatter.6.cloned.1.call-done = f32[1024,32]{0,1:T(8,128)} async-done(((f32[1024,256]{0,1:T(8,128)}), f32[1024,32]{0,1:T(8,128)}) %reduce-scatter.6.cloned.1.call-update) | async-done | bytes 131088 | tf_op jit(solution)/shard_map/reduce_scatter | solution.py:119
  455.9 1.5 multiply_convert_fusion.2
  457.4 147.8 %reduce-scatter.4.cloned.1.call-done = f32[128,256]{1,0:T(8,128)} async-done(((f32[4096,256]{1,0:T(8,128)}), f32[128,256]{1,0:T(8,128)}) %reduce-scatter.4.cloned.1.call-update) | async-done | bytes 131088 | tf_op jit(solution)/shard_map/reduce_scatter | solution.py:117
  605.2 1.5 multiply_convert_fusion.3
  (150 shorter events, 57.2 us)
Async XLA Ops:
  7.2 50.2 %copy-start.1 = (bf16[1024,32]{0,1:T(8,128)(2,1)S(1)}, bf16[1024,32]{0,1:T(8,128)(2,1)}, u32[]{:S(2)}) copy-start(bf16[1024,32]{0,1:T(8,128)(2,1)} %param.10) | copy-start | bytes 196612
  7.2 187.1 %all-gather.3.cloned.1.call-start = ((), (), s32[]{:S(2)}) async-start(), calls=%async_computation.3 | async-start | bytes 2162688 | tf_op jit(solution)/shard_map/all_gather | solution.py:107
  7.9 186.3 %all-gather.5.cloned.1.call-start = ((), (), s32[]{:S(2)}) async-start(), calls=%async_computation.4 | async-start | bytes 2162688 | tf_op jit(solution)/shard_map/all_gather | solution.py:108
  8.7 360.1 %reduce-scatter.8.cloned.1.call-start = ((), (), s32[]{:S(2)}) async-start(), calls=%async_computation.7 | async-start | bytes 1179648 | tf_op jit(solution)/shard_map/reduce_scatter | solution.py:120
  103.6 52.7 %copy-start.2 = (f32[2,128]{1,0:T(2,128)S(1)}, f32[2,128]{1,0:T(2,128)}, u32[]{:S(2)}) copy-start(f32[2,128]{1,0:T(2,128)} %param.13) | copy-start | bytes 3076
  281.2 1.0 copy-start
  282.2 173.6 %reduce-scatter.6.cloned.1.call-start = ((), (), s32[]{:S(2)}) async-start(), calls=%async_computation.6 | async-start | bytes 1179648 | tf_op jit(solution)/shard_map/reduce_scatter | solution.py:119
  282.8 322.4 %reduce-scatter.4.cloned.1.call-start = ((), (), s32[]{:S(2)}) async-start(), calls=%async_computation.5 | async-start | bytes 4325376 | tf_op jit(solution)/shard_map/reduce_scatter | solution.py:117
Sparse Core Ops, SparseCore 0:
  9.9 63.0 all-gather.2
  74.8 60.6 all-gather.4
  282.3 86.4 reduce-scatter.7
  373.1 82.7 reduce-scatter.5
  458.2 146.9 reduce-scatter.3
where the time goes:
time: 614 us; the launch traced here: 613 us
  waiting for transfers between devices  321 us (52%)
  blocking collectives  182 us (30%)
  matrix products  39.4 us (6%)
  other arithmetic  28.6 us (5%)
  local copies, waits for them, and re-layouts  27.7 us (5%)
  between operations  13.9 us (2%)
    reduce_scatter x1, waiting for transfers between devices, per_device(): lax.psum_scatter(query_terms, 'col', scatter_dimension=0, tiled=True)  148 us
    reduce_scatter x1, waiting for transfers between devices, per_device(): lax.psum_scatter(key_sum, 'row', scatter_dimension=1, tiled=True)  85.5 us
    reduce_scatter x1, waiting for transfers between devices, per_device(): lax.psum_scatter(value_sum, 'row', scatter_dimension=1, tiled=True)  85.4 us
    all_gather x1, blocking collectives, per_device(): lax.all_gather(delta, 'col', axis=1, tiled=True)  50.5 us
    all_gather x1, blocking collectives, per_device(): lax.all_gather(keys, 'row', axis=1, tiled=True)  47.4 us
    all_gather x1, blocking collectives, per_device(): lax.all_gather(values, 'row', axis=1, tiled=True)  45.8 us
    all_gather x1, blocking collectives, per_device(): lax.all_gather(lse, 'col', axis=1, tiled=True)  37.9 us
    add x8, other arithmetic, advance(): return ((key_sum + key_term, value_sum + value_term), query_term)  22.6 us
  transfers between devices with their start and end apart: 5, of which 3 were waited for; matrix products, arithmetic and copies ran while one was open for 1% of the time, Pallas kernels for 0%

commit v1 on v0

--- a/solution.py
+++ b/solution.py
@@ -99,9 +99,21 @@
     head_dim = queries.shape[1] // head_total
     scaling = head_dim ** (-0.5)
     delta = head_delta(d_out, outputs, head_total, head_dim)
+
+    def begin_sheets_in(net_axis, message):
+        return jnp.concatenate(
+            lax.all_to_all(
+                jnp.stack([message for _ in range(lax.axis_size(net_axis))], axis=0),
+                axis_name=net_axis,
+                split_axis=0,
+                concat_axis=0,
+            ),
+            1,
+        )
+
     key_all, value_all = (
         lax.all_gather(keys, "row", axis=1, tiled=True),
-        lax.all_gather(values, "row", axis=1, tiled=True),
+        begin_sheets_in("row", values),
     )
     query_all, grad_all = (
         lax.all_gather(queries, "col", axis=0, tiled=True),

time: 614 us -> 584 us (0.951)
  blocking collectives: 182 us -> 137 us
  starting transfers between devices: 0.19 us -> 11.7 us
    all_gather x1 -> x0, blocking collectives: 45.8 us -> none  [per_device(): lax.all_gather(values, 'row', axis=1, tiled=True)]
    all_to_all x0 -> x1, starting transfers between devices: none -> 11.5 us  [begin_sheets_in(): lax.all_to_all(jnp.stack([message for _ in range(lax.axis_size(net_axis))...]
  transfers between devices with their start and end apart: 5 -> 6, of which waited for: 3 -> 3; matrix products, arithmetic and copies ran while one was open for 1% -> 1% of each run, Pallas kernels for 0% -> 0%
where the time goes in v1:
time: 584 us; the launch traced here: 582 us
  waiting for transfers between devices  322 us (55%)
  blocking collectives  137 us (23%)
  matrix products  39.4 us (7%)
  local copies, waits for them, and re-layouts  29.4 us (5%)
  other arithmetic  28.6 us (5%)
  between operations  13.8 us (2%)
  starting transfers between devices  11.7 us (2%)
    reduce_scatter x1, waiting for transfers between devices, per_device(): lax.psum_scatter(query_terms, 'col', scatter_dimension=0, tiled=True)  148 us
    reduce_scatter x1, waiting for transfers between devices, per_device(): lax.psum_scatter(value_sum, 'row', scatter_dimension=1, tiled=True)  86 us
    reduce_scatter x1, waiting for transfers between devices, per_device(): lax.psum_scatter(key_sum, 'row', scatter_dimension=1, tiled=True)  85.6 us
    all_gather x1, blocking collectives, per_device(): lax.all_gather(delta, 'col', axis=1, tiled=True)  50.8 us
    all_gather x1, blocking collectives, per_device(): lax.all_gather(keys, 'row', axis=1, tiled=True)  48 us
    all_gather x1, blocking collectives, per_device(): lax.all_gather(lse, 'col', axis=1, tiled=True)  37.9 us
    add x8, other arithmetic, advance(): return ((key_sum + key_term, value_sum + value_term), query_term)  22.6 us
    squeeze x16, local copies, waits for them, and re-layouts, query_pass(): lax.scan(advance, (empty_sums, empty_sums), block_inputs)  15.6 us
  transfers between devices with their start and end apart: 6, of which 3 were waited for; matrix products, arithmetic and copies ran while one was open for 1% of the time, Pallas kernels for 0%

profile of v1, /device:TPU:8, one launch (start us, length us, event | category | flops | bytes accessed | tf_op | source)
XLA Modules:
  0.0 582.4 jit_solution(5088837384334289093)
XLA Ops:
  8.7 1.7 stack.2
  10.3 11.5 %all-to-all-start = ((bf16[8,1024,32]{1,2,0:T(8,128)(2,1)}), bf16[8,1024,32]{1,2,0:T(8,128)(2,1)S(1)}, u32[]{:S(2)}, u32[]{:S(2)}) async-start(bf16[8,1024,32]{1,2,0:T(8,128)(2,1)} %stack.2), calls=%async_computation | async-start | bytes 1048576 | tf_op jit(solution)/shard_map/all_to_all | solution.py:105
  22.9 48.0 %all_gather.16 = bf16[1024,256]{0,1:T(8,128)(2,1)S(1)} all-gather(bf16[1024,32]{0,1:T(8,128)(2,1)S(1)} %copy-done.1), channel_id=1, replica_groups=mesh['row'=8,'col'=32] {'row'}, dimensions={1}, use_global_device_ids=true | all-gather | bytes 589824 | tf_op jit(solution)/shard_map/all_gather | solution.py:115
  71.3 50.8 %all_gather.19 = f32[2,4096]{0,1:T(8,128)} all-gather(f32[2,128]{0,1:T(8,128)S(1)} %bitcast.59), channel_id=1, replica_groups=mesh['row'=8,'col'=32] {'col'}, dimensions={1}, use_global_device_ids=true | all-gather | bytes 33792 | tf_op jit(solution)/shard_map/all_gather | solution.py:124
  122.1 2.2 copy.19
  124.3 37.9 %all_gather.17 = f32[2,4096]{1,0:T(2,128)S(1)} all-gather(f32[2,128]{1,0:T(2,128)S(1)} %copy-done.2), channel_id=1, replica_groups=mesh['row'=8,'col'=32] {'col'}, dimensions={1}, use_global_device_ids=true | all-gather | bytes 33792 | tf_op jit(solution)/shard_map/all_gather | solution.py:123
  162.5 87.2 %while.15 = (s32[]{:T(128)}, f32[1024,256]{0,1:T(8,128)}, f32[1024,256]{0,1:T(8,128)S(1)}, f32[8,512,256]{2,1,0:T(8,128)}, bf16[8,512,256]{2,1,0:T(8,128)(2,1)},...) while((s32[]{:T(128)}, f32[1024,256]{0,1:T(8,128)}, ...), condition=%wide.region_2.3_spmd.clone, body=%wide.region_1.2_spmd.clone.sunk | while | flops 1352269824 | bytes 34631860 | solution.py:87
  162.6 1.0 dynamic-slice_bitcast_fusion.5
  163.6 1.0 dynamic-slice_bitcast_fusion.4
  169.5 1.8 maximum_add_fusion.3
  172.4 1.0 dynamic-slice_bitcast_fusion.5
  173.4 1.0 dynamic-slice_bitcast_fusion.4
  179.3 3.0 maximum_add_fusion.3
  183.4 1.0 dynamic-slice_bitcast_fusion.5
  184.4 1.0 dynamic-slice_bitcast_fusion.4
  190.4 3.0 maximum_add_fusion.3
  194.5 1.0 dynamic-slice_bitcast_fusion.5
  195.5 1.0 dynamic-slice_bitcast_fusion.4
  201.4 3.0 maximum_add_fusion.3
  206.5 1.0 dynamic-slice_bitcast_fusion.4
  212.5 3.0 maximum_add_fusion.3
  216.6 1.0 dynamic-slice_bitcast_fusion.5
  223.5 3.0 maximum_add_fusion.3
  234.6 3.0 maximum_add_fusion.3
  238.7 1.0 dynamic-slice_bitcast_fusion.5
  245.6 3.0 maximum_add_fusion.3
  251.8 86.0 %reduce-scatter.8.cloned.1.call-done = f32[1024,32]{0,1:T(8,128)} async-done(((f32[1024,256]{0,1:T(8,128)}), f32[1024,32]{0,1:T(8,128)}) %reduce-scatter.8.cloned.1.call-update) | async-done | bytes 131088 | tf_op jit(solution)/shard_map/reduce_scatter | solution.py:132
  337.9 1.5 convert_element_type.31
  339.4 85.6 %reduce-scatter.6.cloned.1.call-done = f32[1024,32]{0,1:T(8,128)} async-done(((f32[1024,256]{0,1:T(8,128)}), f32[1024,32]{0,1:T(8,128)}) %reduce-scatter.6.cloned.1.call-update) | async-done | bytes 131088 | tf_op jit(solution)/shard_map/reduce_scatter | solution.py:131
  425.0 1.5 multiply_convert_fusion.2
  426.5 147.8 %reduce-scatter.4.cloned.1.call-done = f32[128,256]{1,0:T(8,128)} async-done(((f32[4096,256]{1,0:T(8,128)}), f32[128,256]{1,0:T(8,128)}) %reduce-scatter.4.cloned.1.call-update) | async-done | bytes 131088 | tf_op jit(solution)/shard_map/reduce_scatter | solution.py:129
  574.4 1.5 multiply_convert_fusion.3
  (152 shorter events, 58.2 us)
Async XLA Ops:
  7.2 15.7 %copy-start.1 = (bf16[1024,32]{0,1:T(8,128)(2,1)S(1)}, bf16[1024,32]{0,1:T(8,128)(2,1)}, u32[]{:S(2)}) copy-start(bf16[1024,32]{0,1:T(8,128)(2,1)} %param.9) | copy-start | bytes 196612
  7.2 155.3 %all-gather.3.cloned.1.call-start = ((), (), s32[]{:S(2)}) async-start(), calls=%async_computation.4 | async-start | bytes 2162688 | tf_op jit(solution)/shard_map/all_gather | solution.py:119
  7.9 154.6 %all-gather.5.cloned.1.call-start = ((), (), s32[]{:S(2)}) async-start(), calls=%async_computation.5 | async-start | bytes 2162688 | tf_op jit(solution)/shard_map/all_gather | solution.py:120
  10.3 151.9 %all-to-all-start = ((bf16[8,1024,32]{1,2,0:T(8,128)(2,1)}), bf16[8,1024,32]{1,2,0:T(8,128)(2,1)S(1)}, u32[]{:S(2)}, u32[]{:S(2)}) async-start(bf16[8,1024,32]{1,2,0:T(8,128)(2,1)} %stack.2), calls=%async_computation | async-start | bytes 1048576 | tf_op jit(solution)/shard_map/all_to_all | solution.py:105
  21.9 316.0 %reduce-scatter.8.cloned.1.call-start = ((), (), s32[]{:S(2)}) async-start(), calls=%async_computation.8 | async-start | bytes 1179648 | tf_op jit(solution)/shard_map/reduce_scatter | solution.py:132
  71.3 53.0 %copy-start.2 = (f32[2,128]{1,0:T(2,128)S(1)}, f32[2,128]{1,0:T(2,128)}, u32[]{:S(2)}) copy-start(f32[2,128]{1,0:T(2,128)} %param.13) | copy-start | bytes 3076
  249.7 1.0 copy-start
  250.7 174.3 %reduce-scatter.6.cloned.1.call-start = ((), (), s32[]{:S(2)}) async-start(), calls=%async_computation.7 | async-start | bytes 1179648 | tf_op jit(solution)/shard_map/reduce_scatter | solution.py:131
  251.2 323.1 %reduce-scatter.4.cloned.1.call-start = ((), (), s32[]{:S(2)}) async-start(), calls=%async_computation.6 | async-start | bytes 4325376 | tf_op jit(solution)/shard_map/reduce_scatter | solution.py:129
Sparse Core Ops, SparseCore 0:
  9.9 67.4 all-gather.2
  79.2 64.2 all-gather.4
  250.8 87.0 reduce-scatter.7
  342.2 82.7 reduce-scatter.5
  427.4 146.9 reduce-scatter.3
